TPU v7x, 256 devices: a whole 4x4x8 slice. The times are simulated.
256 devices in a mesh: dp: 32 (over x, y, core), tensor: 8 (over z).
Axes of the slice: x: 4, y: 4, z: 8, core: 2. Of those that a mesh axis runs over, the one named last changes fastest.
Arguments:
- inputs: bfloat16 [32768, 8192], P('dp', 'tensor'), may hold values from -6 to 6
- frozen_value_weight: bfloat16 [8192, 1024], P('tensor'), may hold values from -0.0625 to 0.0625
- adapter_down_weight: bfloat16 [512, 8192, 64], P('dp', 'tensor'), may hold values from -0.0625 to 0.0625
- adapter_up_weight: bfloat16 [512, 64, 1024], P('dp', None, 'tensor'), may hold values from -0.75 to 0.75
- adapter_per_block: int32 [256], P('dp'), may hold values from 0 to 511, as said below
- adapter_storage_index: int32 [512], replicated, may hold values from 0 to 511, as said below
- value_gradient: bfloat16 [32768, 1024], P('dp', 'tensor'), may hold values from -6 to 6
Outputs:
- values: bfloat16 [32768, 1024], P('dp', 'tensor')
- grad_inputs: bfloat16 [32768, 8192], P('dp', 'tensor')
- grad_down: bfloat16 [512, 8192, 64], P('dp', 'tensor')
- grad_up: bfloat16 [512, 64, 1024], P('dp', None, 'tensor')
Inputs may be any that keep to these rules, and one draw needn't show every extreme that they name: Adapter a is kept by data device adapter_storage_index[a] // 16; adapter_storage_index is a permutation. `adapter_per_block`: the 8 blocks of one data device use adapters kept by pairwise different data devices; in every draw there is one data device whose adapters are used by a block of every data device, so that keeper serves all 32 data devices.
All inputs are finite; a program needn't handle non-finite values.
Results may differ from a plain program's by a relative error of at most 0.0054.
Values may be sent and summed in bfloat16 or wider, within the bound.
A program may use at most 128 MiB of HBM per device.

v0:
```python
import jax
import jax.numpy as jnp
from jax import lax
from jax.sharding import PartitionSpec as P

BLOCK = 128
adapter_scale = 0.5


def exchange(pieces):
    return lax.all_to_all(pieces, "dp", split_axis=0, concat_axis=0, tiled=True)


def cut(mats, parts):
    m, rank, width = mats.shape
    rows = rank // parts
    return mats.reshape(m, parts, rows * width).swapaxes(0, 1)


def join(pieces, width):
    parts, m, size = pieces.shape
    return pieces.swapaxes(0, 1).reshape(m, parts * (size // width), width)


def on_device(
    inputs,
    frozen_value_weight,
    adapter_down_weight,
    adapter_up_weight,
    adapter_per_block,
    adapter_storage_index,
    value_gradient,
):
    n = lax.axis_size("dp")
    nblocks = adapter_per_block.shape[0]
    kept = adapter_down_weight.shape[0]
    total = adapter_storage_index.shape[0]
    rows = inputs.shape[0]
    feat = inputs.shape[1]
    columns = value_gradient.shape[1]
    f32, bf16 = (jnp.float32, jnp.bfloat16)
    up_table = exchange(cut(adapter_up_weight, n)).reshape(total, -1)
    down_table = exchange(cut(adapter_down_weight.swapaxes(1, 2), n)).reshape(total, -1)
    spot = adapter_storage_index[adapter_per_block]
    spots = lax.all_gather(spot, "dp", axis=0, tiled=True)
    pick = (spots[:, None] == jnp.arange(total, dtype=jnp.int32)[None, :]).astype(bf16)

    def fetch(table, width):
        chosen = jnp.dot(pick, table, preferred_element_type=f32).astype(bf16)
        return join(exchange(chosen.reshape(n, nblocks, -1)), width)

    def give(terms, width):
        pieces = exchange(cut(terms, n)).reshape(n * nblocks, -1)
        sums = lax.dot_general(
            pick, pieces, (((0,), (0,)), ((), ())), preferred_element_type=f32
        ).astype(bf16)
        return join(exchange(sums.reshape(n, kept, -1)), width)

    block_up = fetch(up_table, columns)
    block_down = fetch(down_table, feat)
    x_blocks = inputs.reshape(nblocks, BLOCK, feat)
    dy_blocks = value_gradient.reshape(nblocks, BLOCK, columns)
    partial_low_gradient = adapter_scale * jnp.einsum(
        "bnk,brk->bnr", dy_blocks, block_up, preferred_element_type=f32
    )
    low_rank_gradient = lax.psum(partial_low_gradient, "tensor").astype(bf16)
    term_down = jnp.einsum(
        "bnd,bnr->brd", x_blocks, low_rank_gradient, preferred_element_type=f32
    ).astype(bf16)
    grad_down = give(term_down, feat).swapaxes(1, 2)
    partial_base = jnp.dot(inputs, frozen_value_weight, preferred_element_type=f32)
    frozen_output = lax.psum_scatter(partial_base, "tensor", scatter_dimension=1, tiled=True)
    low_part = jnp.einsum("bnd,brd->bnr", x_blocks, block_down, preferred_element_type=f32)
    low = lax.psum(low_part, "tensor").astype(bf16)
    term_up = jnp.einsum("bnr,bnk->brk", low, dy_blocks, preferred_element_type=f32).astype(bf16)
    grad_up = give(term_up, columns)
    raised_output = jnp.einsum("bnr,brk->bnk", low, block_up, preferred_element_type=f32)
    values = (frozen_output + adapter_scale * raised_output.reshape(rows, columns)).astype(bf16)
    grad_base = lax.dot_general(
        lax.all_gather(value_gradient, "tensor", axis=1, tiled=True),
        frozen_value_weight,
        (((1,), (1,)), ((), ())),
        preferred_element_type=f32,
    )
    back = jnp.einsum("bnr,brd->bnd", low_rank_gradient, block_down, preferred_element_type=f32)
    grad_inputs = (grad_base + back.reshape(rows, feat)).astype(bf16)
    return (values, grad_inputs, grad_down, grad_up)


def solution(mesh):
    return jax.shard_map(
        on_device,
        mesh=mesh,
        in_specs=(
            P("dp", "tensor"),
            P("tensor", None),
            P("dp", "tensor", None),
            P("dp", None, "tensor"),
            P("dp"),
            P(),
            P("dp", "tensor"),
        ),
        out_specs=(
            P("dp", "tensor"),
            P("dp", "tensor"),
            P("dp", "tensor", None),
            P("dp", None, "tensor"),
        ),
        check_vma=False,
    )
```

profile of v0, /device:TPU:1, one launch (start us, length us, event | category | flops | bytes accessed | tf_op | source)
XLA Modules:
  0.0 258.1 jit_solution(17837545737444184201)
XLA Ops:
  8.8 5.9 %fusion.16 = f32[1024,1024]{1,0:T(8,128)} fusion(bf16[1024,1024]{1,0:T(8,128)(2,1)S(1)} %copy-done, bf16[1024,1024]{1,0:T(8,128)(2,1)} %param.8), kind=kOutput, calls=%fused_computation.33 | convolution fusion | flops 2147483648 | bytes 8388608 | tf_op jit(solution)/shard_map/dot_general | solution.py:71
  16.5 8.6 %all-to-all-start.2 = ((bf16[32,16,256]{2,1,0:T(8,128)(2,1)}), bf16[32,16,256]{2,1,0:T(8,128)(2,1)S(1)}, u32[]{:S(2)}, u32[]{:S(2)}) async-start(bf16[32,16,256]{2,1,0:T(8,128)(2,1)} %copy.31), calls=%async_computation.3 | async-start | bytes 524288 | tf_op jit(solution)/shard_map/all_to_all | solution.py:11
  25.1 4.1 %reshape.69 = bf16[16,32,2048]{2,1,0:T(8,128)(2,1)} reshape(bf16[16,64,1024]{2,1,0:T(8,128)(2,1)} %bitcast.69) | data formatting | bytes 4194304 | tf_op jit(solution)/shard_map/reshape | solution.py:17
  29.2 4.1 %copy.29 = bf16[32,16,2048]{2,1,0:T(8,128)(2,1)} copy(bf16[32,16,2048]{2,0,1:T(8,128)(2,1)} %bitcast.64) | data formatting | bytes 4194304 | tf_op jit(solution)/shard_map/transpose | solution.py:17
  34.1 6.7 %all-to-all-start = ((bf16[32,16,2048]{2,1,0:T(8,128)(2,1)}), bf16[32,16,2048]{2,1,0:T(8,128)(2,1)}, u32[]{:S(2)}, u32[]{:S(2)}) async-start(bf16[32,16,2048]{2,1,0:T(8,128)(2,1)} %copy.29), calls=%async_computation.1 | async-start | bytes 4194304 | tf_op jit(solution)/shard_map/all_to_all | solution.py:11
  43.0 31.7 %all-reduce = s32[256]{0:T(256)S(1)} all-reduce(s32[256]{0:T(256)S(1)} %dynamic-update-slice), channel_id=2, replica_groups=mesh['dp'=32,'tensor'=8] {'dp'}, use_global_device_ids=true, to_apply=%add | all-reduce | flops 256 | bytes 2048
  75.7 6.9 %all-to-all-start.3 = ((bf16[32,8,256]{2,1,0:T(8,128)(2,1)}), bf16[32,8,256]{2,1,0:T(8,128)(2,1)S(1)}, u32[]{:S(2)}, u32[]{:S(2)}) async-start(bf16[32,8,256]{2,1,0:T(8,128)(2,1)} %fusion.3), calls=%async_computation.4 | async-start | bytes 262144 | tf_op jit(solution)/shard_map/all_to_all | solution.py:11
  82.6 3.3 %fusion.1 = bf16[32,8,2048]{2,1,0:T(8,128)(2,1)} fusion(bf16[512,2048]{1,0:T(8,128)(2,1)} %bitcast.3, s32[256]{0:T(256)S(1)} %all-reduce), kind=kOutput, calls=%fused_computation.5 | convolution fusion | flops 537526272 | bytes 3146752 | tf_op jit(solution)/shard_map/dot_general | solution.py:49
  85.9 4.5 %all-to-all-done.3 = bf16[32,8,256]{2,1,0:T(8,128)(2,1)S(1)} async-done(((bf16[32,8,256]{2,1,0:T(8,128)(2,1)}), bf16[32,8,256]{2,1,0:T(8,128)(2,1)S(1)}, u32[]{:S(2)}, u32[]{:S(2)}) %all-to-all-start.3) | async-done | bytes 131104 | tf_op jit(solution)/shard_map/all_to_all | solution.py:11
  90.4 4.0 %all-to-all-start.1 = ((bf16[32,8,2048]{2,1,0:T(8,128)(2,1)}), bf16[32,8,2048]{2,1,0:T(8,128)(2,1)S(1)}, u32[]{:S(2)}, u32[]{:S(2)}) async-start(bf16[32,8,2048]{2,1,0:T(8,128)(2,1)} %fusion.1), calls=%async_computation.2 | async-start | bytes 2097152 | tf_op jit(solution)/shard_map/all_to_all | solution.py:11
  97.1 14.4 %all-to-all-done.1 = bf16[32,8,2048]{2,1,0:T(8,128)(2,1)S(1)} async-done(((bf16[32,8,2048]{2,1,0:T(8,128)(2,1)}), bf16[32,8,2048]{2,1,0:T(8,128)(2,1)S(1)}, u32[]{:S(2)}, u32[]{:S(2)}) %all-to-all-start.1) | async-done | bytes 1048608 | tf_op jit(solution)/shard_map/all_to_all | solution.py:11
  115.9 33.5 %all-reduce.3 = (bf16[8,128,64]{1,2,0:T(8,128)(2,1)}, bf16[8,128,64]{1,2,0:T(8,128)(2,1)}) all-reduce(f32[8,128,64]{1,2,0:T(8,128)} %convolution_bitcast_fusion, f32[8,128,64]{1,2,0:T(8,128)} %fusion.2), channel_id=1, replica_groups=mesh['dp'=32,'tensor'=8] {'tensor'}, use_global_device_ids=true, to_apply=%region_1.0 | all-reduce | flops 131072 | bytes 786432 | tf_op jit(solution)/shard_map/psum | solution.py:74
  152.9 10.8 %all-to-all-start.6 = ((bf16[32,8,256]{2,1,0:T(8,128)(2,1)}), bf16[32,8,256]{2,1,0:T(8,128)(2,1)S(1)}, u32[]{:S(2)}, u32[]{:S(2)}) async-start(bf16[32,8,256]{2,1,0:T(8,128)(2,1)} %bitcast.60), calls=%async_computation.7 | async-start | bytes 262144 | tf_op jit(solution)/shard_map/all_to_all | solution.py:11
  171.4 7.0 %all-to-all-start.4 = ((bf16[32,8,2048]{2,1,0:T(8,128)(2,1)}), bf16[32,8,2048]{2,1,0:T(8,128)(2,1)}, u32[]{:S(2)}, u32[]{:S(2)}) async-start(bf16[32,8,2048]{2,1,0:T(8,128)(2,1)} %bitcast.66), calls=%async_computation.5 | async-start | bytes 2097152 | tf_op jit(solution)/shard_map/all_to_all | solution.py:11
  179.5 15.8 %all-to-all-done.4 = bf16[32,8,2048]{2,1,0:T(8,128)(2,1)} async-done(((bf16[32,8,2048]{2,1,0:T(8,128)(2,1)}), bf16[32,8,2048]{2,1,0:T(8,128)(2,1)}, u32[]{:S(2)}, u32[]{:S(2)}) %all-to-all-start.4) | async-done | bytes 1048608 | tf_op jit(solution)/shard_map/all_to_all | solution.py:11
  195.4 4.0 %all-to-all-start.7 = ((bf16[32,16,256]{2,1,0:T(8,128)(2,1)}), bf16[32,16,256]{2,1,0:T(8,128)(2,1)S(1)}, u32[]{:S(2)}, u32[]{:S(2)}) async-start(bf16[32,16,256]{2,1,0:T(8,128)(2,1)} %bitcast.72), calls=%async_computation.8 | async-start | bytes 524288 | tf_op jit(solution)/shard_map/all_to_all | solution.py:11
  199.3 3.4 %convolution_convert_fusion = bf16[512,2048]{1,0:T(8,128)(2,1)} fusion(bf16[32,8,2048]{2,1,0:T(8,128)(2,1)} %all-to-all-done.4, s32[256]{0:T(256)S(1)} %all-reduce), kind=kOutput, calls=%fused_computation.3 | convolution fusion | flops 538050560 | bytes 3146752 | tf_op jit(solution)/shard_map/dot_general | solution.py:54
  202.7 5.6 %all-to-all-done.7 = bf16[32,16,256]{2,1,0:T(8,128)(2,1)S(1)} async-done(((bf16[32,16,256]{2,1,0:T(8,128)(2,1)}), bf16[32,16,256]{2,1,0:T(8,128)(2,1)S(1)}, u32[]{:S(2)}, u32[]{:S(2)}) %all-to-all-start.7) | async-done | bytes 262176 | tf_op jit(solution)/shard_map/all_to_all | solution.py:11
  208.3 4.6 %all-to-all-start.5 = ((bf16[32,16,2048]{2,1,0:T(8,128)(2,1)}), bf16[32,16,2048]{2,1,0:T(8,128)(2,1)}, u32[]{:S(2)}, u32[]{:S(2)}) async-start(bf16[32,16,2048]{2,1,0:T(8,128)(2,1)} %bitcast.63), calls=%async_computation.6 | async-start | bytes 4194304 | tf_op jit(solution)/shard_map/all_to_all | solution.py:11
  214.9 3.6 %fusion.17 = f32[8,128,1024]{2,1,0:T(8,128)} fusion(bf16[8,128,64]{1,2,0:T(8,128)(2,1)} %get-tuple-element.5, bf16[8,64,1024]{2,1,0:T(8,128)(2,1)S(1)} %reshape.72), kind=kOutput, calls=%fused_computation.34 | convolution fusion | flops 134217728 | bytes 5373952 | tf_op jit(solution)/shard_map/bnr,brd->bnd/dot_general | solution.py:85
  219.4 7.2 %fusion = bf16[1024,1024]{1,0:T(8,128)(2,1)} fusion(f32[8,128,1024]{2,1,0:T(8,128)} %fusion.17, bf16[1024,1024]{1,0:T(8,128)(2,1)} %all-gather.3.cloned.1.call-done, bf16[1024,1024]{1,0:T(8,128)(2,1)} %param.8), kind=kOutput, calls=%fused_computation.2 | convolution fusion | flops 2149580800 | bytes 10485760 | tf_op jit(solution)/shard_map/dot_general | solution.py:79
  226.5 14.7 %all-to-all-done.5 = bf16[32,16,2048]{2,1,0:T(8,128)(2,1)} async-done(((bf16[32,16,2048]{2,1,0:T(8,128)(2,1)}), bf16[32,16,2048]{2,1,0:T(8,128)(2,1)}, u32[]{:S(2)}, u32[]{:S(2)}) %all-to-all-start.5) | async-done | bytes 2097184 | tf_op jit(solution)/shard_map/all_to_all | solution.py:11
  241.3 4.1 %copy.34 = bf16[16,32,2048]{2,1,0:T(8,128)(2,1)} copy(bf16[16,32,2048]{2,0,1:T(8,128)(2,1)} %bitcast.19) | data formatting | bytes 4194304 | tf_op jit(solution)/shard_map/transpose | solution.py:22
  245.4 4.1 %reshape.83 = bf16[16,64,1024]{2,1,0:T(8,128)(2,1)} reshape(bf16[16,32,2048]{2,1,0:T(8,128)(2,1)} %copy.34) | data formatting | bytes 4194304 | tf_op jit(solution)/shard_map/reshape | solution.py:22
  (49 shorter events, 30.8 us)
Async XLA Ops:
  7.2 1.6 copy-start
  7.2 212.2 %all-gather.3.cloned.1.call-start = ((), (), s32[]{:S(2)}) async-start(), calls=%async_computation.10 | async-start | bytes 2359296 | tf_op jit(solution)/shard_map/all_gather | solution.py:80
  7.9 241.6 %reduce-scatter.2.cloned.1.call-start = ((), (), s32[]{:S(2)}) async-start(), calls=%async_computation.9 | async-start | bytes 4718592 | tf_op jit(solution)/shard_map/reduce_scatter | solution.py:72
  14.6 0.9 copy-start.4
  16.5 17.6 %all-to-all-start.2 = ((bf16[32,16,256]{2,1,0:T(8,128)(2,1)}), bf16[32,16,256]{2,1,0:T(8,128)(2,1)S(1)}, u32[]{:S(2)}, u32[]{:S(2)}) async-start(bf16[32,16,256]{2,1,0:T(8,128)(2,1)} %copy.31), calls=%async_computation.3 | async-start | bytes 524288 | tf_op jit(solution)/shard_map/all_to_all | solution.py:11
  33.2 7.6 %copy-start.5 = (s32[8]{0:T(128)S(1)}, s32[8]{0:T(128)}, u32[]{:S(2)}) copy-start(s32[8]{0:T(128)} %param.11) | copy-start | bytes 100
  33.3 7.6 %copy-start.1 = (s32[512]{0:T(512)S(1)}, s32[512]{0:T(512)}, u32[]{:S(2)}) copy-start(s32[512]{0:T(512)} %param.12) | copy-start | bytes 6148
  33.3 8.3 %copy-start.6 = (u32[256]{0:T(256)S(1)}, u32[256]{0:T(256)}, u32[]{:S(2)}) copy-start(u32[256]{0:T(256)} %constant.12) | copy-start | bytes 3076
  34.1 41.6 %all-to-all-start = ((bf16[32,16,2048]{2,1,0:T(8,128)(2,1)}), bf16[32,16,2048]{2,1,0:T(8,128)(2,1)}, u32[]{:S(2)}, u32[]{:S(2)}) async-start(bf16[32,16,2048]{2,1,0:T(8,128)(2,1)} %copy.29), calls=%async_computation.1 | async-start | bytes 4194304 | tf_op jit(solution)/shard_map/all_to_all | solution.py:11
  75.7 14.7 %all-to-all-start.3 = ((bf16[32,8,256]{2,1,0:T(8,128)(2,1)}), bf16[32,8,256]{2,1,0:T(8,128)(2,1)S(1)}, u32[]{:S(2)}, u32[]{:S(2)}) async-start(bf16[32,8,256]{2,1,0:T(8,128)(2,1)} %fusion.3), calls=%async_computation.4 | async-start | bytes 262144 | tf_op jit(solution)/shard_map/all_to_all | solution.py:11
  85.9 10.1 %copy-start.2 = (bf16[1024,128]{1,0:T(8,128)(2,1)S(1)}, bf16[1024,128]{1,0:T(8,128)(2,1)}, u32[]{:S(2)}) copy-start(bf16[1024,128]{1,0:T(8,128)(2,1)} %param.13) | copy-start | bytes 786436
  90.4 21.0 %all-to-all-start.1 = ((bf16[32,8,2048]{2,1,0:T(8,128)(2,1)}), bf16[32,8,2048]{2,1,0:T(8,128)(2,1)S(1)}, u32[]{:S(2)}, u32[]{:S(2)}) async-start(bf16[32,8,2048]{2,1,0:T(8,128)(2,1)} %fusion.1), calls=%async_computation.2 | async-start | bytes 2097152 | tf_op jit(solution)/shard_map/all_to_all | solution.py:11
  152.9 18.5 %all-to-all-start.6 = ((bf16[32,8,256]{2,1,0:T(8,128)(2,1)}), bf16[32,8,256]{2,1,0:T(8,128)(2,1)S(1)}, u32[]{:S(2)}, u32[]{:S(2)}) async-start(bf16[32,8,256]{2,1,0:T(8,128)(2,1)} %bitcast.60), calls=%async_computation.7 | async-start | bytes 262144 | tf_op jit(solution)/shard_map/all_to_all | solution.py:11
  171.4 24.0 %all-to-all-start.4 = ((bf16[32,8,2048]{2,1,0:T(8,128)(2,1)}), bf16[32,8,2048]{2,1,0:T(8,128)(2,1)}, u32[]{:S(2)}, u32[]{:S(2)}) async-start(bf16[32,8,2048]{2,1,0:T(8,128)(2,1)} %bitcast.66), calls=%async_computation.5 | async-start | bytes 2097152 | tf_op jit(solution)/shard_map/all_to_all | solution.py:11
  195.4 13.0 %all-to-all-start.7 = ((bf16[32,16,256]{2,1,0:T(8,128)(2,1)}), bf16[32,16,256]{2,1,0:T(8,128)(2,1)S(1)}, u32[]{:S(2)}, u32[]{:S(2)}) async-start(bf16[32,16,256]{2,1,0:T(8,128)(2,1)} %bitcast.72), calls=%async_computation.8 | async-start | bytes 524288 | tf_op jit(solution)/shard_map/all_to_all | solution.py:11
  208.3 33.0 %all-to-all-start.5 = ((bf16[32,16,2048]{2,1,0:T(8,128)(2,1)}), bf16[32,16,2048]{2,1,0:T(8,128)(2,1)}, u32[]{:S(2)}, u32[]{:S(2)}) async-start(bf16[32,16,2048]{2,1,0:T(8,128)(2,1)} %bitcast.63), calls=%async_computation.6 | async-start | bytes 4194304 | tf_op jit(solution)/shard_map/all_to_all | solution.py:11
  245.4 4.1 %copy-start.3 = (f32[8,128,128]{2,1,0:T(8,128)S(1)}, f32[8,128,128]{2,1,0:T(8,128)}, u32[]{:S(2)}) copy-start(f32[8,128,128]{2,1,0:T(8,128)} %convolution_multiply_fusion) | copy-start | bytes 1572868
Sparse Core Ops, SparseCore 0:
  9.7 47.7 all-gather.2
  60.1 57.5 reduce-scatter.1
where the time goes:
time: 260 us; the launch traced here: 258 us
  blocking collectives  65.2 us (25%)
  waiting for transfers between devices  57 us (22%)
  starting transfers between devices  52.5 us (20%)
  matrix products  34 us (13%)
  local copies, waits for them, and re-layouts  32.6 us (13%)
  between operations  14.9 us (6%)
    all_to_all x8, waiting for transfers between devices, exchange(): return lax.all_to_all(pieces, 'dp', split_axis=0, concat_axis=0, tiled=True)  56.3 us
    all_to_all x8, starting transfers between devices, exchange(): return lax.all_to_all(pieces, 'dp', split_axis=0, concat_axis=0, tiled=True)  52.5 us
    psum x1, blocking collectives, on_device(): low = lax.psum(low_part, 'tensor').astype(bf16)  33.5 us
    unnamed x1, blocking collectives  31.7 us
    reshape x6, local copies, waits for them, and re-layouts, cut(): return mats.reshape(m, parts, rows * width).swapaxes(0, 1)  10.8 us
    reshape x4, local copies, waits for them, and re-layouts, join(): return pieces.swapaxes(0, 1).reshape(m, parts * (size // width), width)  7.29 us
    dot_general x1, matrix products, on_device(): lax.dot_general(lax.all_gather(value_gradient, 'tensor', axis=1, tiled=Tr...  7.15 us
    transpose x4, local copies, waits for them, and re-layouts, join(): return pieces.swapaxes(0, 1).reshape(m, parts * (size // width), width)  6.4 us
  transfers between devices with their start and end apart: 10, of which 7 were waited for; matrix products, arithmetic and copies ran while one was open for 25% of the time, Pallas kernels for 0%

commit v1 on v0

--- a/solution.py
+++ b/solution.py
@@ -71,7 +71,7 @@
     partial_base = jnp.dot(inputs, frozen_value_weight, preferred_element_type=f32)
     frozen_output = lax.psum_scatter(partial_base, "tensor", scatter_dimension=1, tiled=True)
     low_part = jnp.einsum("bnd,brd->bnr", x_blocks, block_down, preferred_element_type=f32)
-    low = lax.psum(low_part, "tensor").astype(bf16)
+    low = jnp.sum(lax.all_gather(low_part, "tensor"), axis=0).astype(bf16)
     term_up = jnp.einsum("bnr,bnk->brk", low, dy_blocks, preferred_element_type=f32).astype(bf16)
     grad_up = give(term_up, columns)
     raised_output = jnp.einsum("bnr,brk->bnk", low, block_up, preferred_element_type=f32)

time: 260 us -> 268 us (1.031)
  blocking collectives: 65.2 us -> 137 us
  waiting for transfers between devices: 57 us -> 24.5 us
  starting transfers between devices: 52.5 us -> 25.5 us
  matrix products: 34 us -> 29.5 us
    all_to_all x0 -> x4, blocking collectives: none -> 74 us  [exchange(): return lax.all_to_all(pieces, 'dp', split_axis=0, concat_axis=0, tiled=True)]
    all_to_all x8 -> x4, waiting for transfers between devices: 56.3 us -> 23.8 us  [exchange(): return lax.all_to_all(pieces, 'dp', split_axis=0, concat_axis=0, tiled=True)]
    all_to_all x8 -> x4, starting transfers between devices: 52.5 us -> 25.4 us  [exchange(): return lax.all_to_all(pieces, 'dp', split_axis=0, concat_axis=0, tiled=True)]
  transfers between devices with their start and end apart: 10 -> 7, of which waited for: 7 -> 2; matrix products, arithmetic and copies ran while one was open for 25% -> 18% of each run, Pallas kernels for 0% -> 0%
where the time goes in v1:
time: 268 us; the launch traced here: 267 us
  blocking collectives  137 us (51%)
  local copies, waits for them, and re-layouts  32 us (12%)
  matrix products  29.5 us (11%)
  starting transfers between devices  25.5 us (10%)
  waiting for transfers between devices  24.5 us (9%)
  between operations  14.6 us (5%)
  other arithmetic  4.21 us (2%)
    all_to_all x4, blocking collectives, exchange(): return lax.all_to_all(pieces, 'dp', split_axis=0, concat_axis=0, tiled=True)  74 us
    unnamed x1, blocking collectives  31.7 us
    psum x1, blocking collectives, on_device(): low_rank_gradient = lax.psum(partial_low_gradient, 'tensor').astype(bf16)  31 us
    all_to_all x4, starting transfers between devices, exchange(): return lax.all_to_all(pieces, 'dp', split_axis=0, concat_axis=0, tiled=True)  25.4 us
    all_to_all x4, waiting for transfers between devices, exchange(): return lax.all_to_all(pieces, 'dp', split_axis=0, concat_axis=0, tiled=True)  23.8 us
    reshape x6, local copies, waits for them, and re-layouts, cut(): return mats.reshape(m, parts, rows * width).swapaxes(0, 1)  11.7 us
    reshape x4, local copies, waits for them, and re-layouts, join(): return pieces.swapaxes(0, 1).reshape(m, parts * (size // width), width)  7.21 us
    dot_general x1, matrix products, on_device(): lax.dot_general(lax.all_gather(value_gradient, 'tensor', axis=1, tiled=Tr...  7.18 us
  transfers between devices with their start and end apart: 7, of which 2 were waited for; matrix products, arithmetic and copies ran while one was open for 18% of the time, Pallas kernels for 0%

profile of v1, /device:TPU:1, one launch (start us, length us, event | category | flops | bytes accessed | tf_op | source)
XLA Modules:
  0.0 267.0 jit_solution(12403803752575560574)
XLA Ops:
  7.2 4.2 %reshape.69 = bf16[16,32,2048]{2,1,0:T(8,128)(2,1)} reshape(bf16[16,64,1024]{2,1,0:T(8,128)(2,1)} %bitcast.71) | data formatting | bytes 4194304 | tf_op jit(solution)/shard_map/reshape | solution.py:17
  11.4 4.1 %copy.29 = bf16[32,16,2048]{2,1,0:T(8,128)(2,1)} copy(bf16[32,16,2048]{2,0,1:T(8,128)(2,1)} %bitcast.65) | data formatting | bytes 4194304 | tf_op jit(solution)/shard_map/transpose | solution.py:17
  15.5 8.8 %all-to-all-start = ((bf16[32,16,2048]{2,1,0:T(8,128)(2,1)}), bf16[32,16,2048]{2,1,0:T(8,128)(2,1)}, u32[]{:S(2)}, u32[]{:S(2)}) async-start(bf16[32,16,2048]{2,1,0:T(8,128)(2,1)} %copy.29), calls=%async_computation.1 | async-start | bytes 4194304 | tf_op jit(solution)/shard_map/all_to_all | solution.py:11
  26.5 31.7 %all-reduce = s32[256]{0:T(256)S(1)} all-reduce(s32[256]{0:T(256)S(1)} %dynamic-update-slice), channel_id=2, replica_groups=mesh['dp'=32,'tensor'=8] {'dp'}, use_global_device_ids=true, to_apply=%add | all-reduce | flops 256 | bytes 2048
  58.2 2.3 fusion.1
  60.5 23.0 %all_to_all.40 = bf16[32,8,2048]{2,1,0:T(8,128)(2,1)S(1)} all-to-all(bf16[32,8,2048]{2,1,0:T(8,128)(2,1)S(1)} %fusion.1), channel_id=1, replica_groups=mesh['dp'=32,'tensor'=8] {'dp'}, dimensions={0} | all-to-all | bytes 2097152 | tf_op jit(solution)/shard_map/all_to_all | solution.py:11
  88.9 5.9 %fusion.16 = f32[1024,1024]{1,0:T(8,128)} fusion(bf16[1024,1024]{1,0:T(8,128)(2,1)S(1)} %copy-done, bf16[1024,1024]{1,0:T(8,128)(2,1)} %param.8), kind=kOutput, calls=%fused_computation.33 | convolution fusion | flops 2147483648 | bytes 8388608 | tf_op jit(solution)/shard_map/dot_general | solution.py:71
  97.7 12.7 %all_to_all.41 = bf16[32,16,256]{2,1,0:T(8,128)(2,1)S(1)} all-to-all(bf16[32,16,256]{2,1,0:T(8,128)(2,1)S(1)} %copy.31), channel_id=1, replica_groups=mesh['dp'=32,'tensor'=8] {'dp'}, dimensions={0} | all-to-all | bytes 524288 | tf_op jit(solution)/shard_map/all_to_all | solution.py:11
  110.7 11.2 %all_to_all.42 = bf16[32,8,256]{2,1,0:T(8,128)(2,1)S(1)} all-to-all(bf16[32,8,256]{2,1,0:T(8,128)(2,1)S(1)} %fusion.3), channel_id=1, replica_groups=mesh['dp'=32,'tensor'=8] {'dp'}, dimensions={0} | all-to-all | bytes 262144 | tf_op jit(solution)/shard_map/all_to_all | solution.py:11
  124.5 31.0 %all-reduce.2 = bf16[8,128,64]{1,2,0:T(8,128)(2,1)} all-reduce(f32[8,128,64]{1,2,0:T(8,128)} %fusion.2), channel_id=1, replica_groups=mesh['dp'=32,'tensor'=8] {'tensor'}, use_global_device_ids=true, to_apply=%region_2.0 | all-reduce | flops 65536 | bytes 393216 | tf_op jit(solution)/shard_map/psum | solution.py:66
  155.6 2.3 convolution_convert_fusion.2
  157.9 2.2 reshape.80
  160.1 1.8 copy.39
  161.9 27.1 %all_to_all.43 = bf16[32,8,2048]{2,1,0:T(8,128)(2,1)S(1)} all-to-all(bf16[32,8,2048]{2,1,0:T(8,128)(2,1)S(1)} %bitcast.67), channel_id=1, replica_groups=mesh['dp'=32,'tensor'=8] {'dp'}, dimensions={0} | all-to-all | bytes 2097152 | tf_op jit(solution)/shard_map/all_to_all | solution.py:11
  189.0 2.2 convolution_convert_fusion
  191.1 4.7 %all-to-all-start.5 = ((bf16[32,16,2048]{2,1,0:T(8,128)(2,1)}), bf16[32,16,2048]{2,1,0:T(8,128)(2,1)}, u32[]{:S(2)}, u32[]{:S(2)}) async-start(bf16[32,16,2048]{2,1,0:T(8,128)(2,1)} %bitcast.64), calls=%async_computation.6 | async-start | bytes 4194304 | tf_op jit(solution)/shard_map/all_to_all | solution.py:11
  195.9 2.4 reduce_sum.9
  201.8 22.3 %all-to-all-done.5 = bf16[32,16,2048]{2,1,0:T(8,128)(2,1)} async-done(((bf16[32,16,2048]{2,1,0:T(8,128)(2,1)}), bf16[32,16,2048]{2,1,0:T(8,128)(2,1)}, u32[]{:S(2)}, u32[]{:S(2)}) %all-to-all-start.5) | async-done | bytes 2097184 | tf_op jit(solution)/shard_map/all_to_all | solution.py:11
  224.1 4.4 %all-to-all-start.6 = ((bf16[32,8,256]{2,1,0:T(8,128)(2,1)}), bf16[32,8,256]{2,1,0:T(8,128)(2,1)S(1)}, u32[]{:S(2)}, u32[]{:S(2)}) async-start(bf16[32,8,256]{2,1,0:T(8,128)(2,1)} %bitcast.61), calls=%async_computation.7 | async-start | bytes 262144 | tf_op jit(solution)/shard_map/all_to_all | solution.py:11
  228.4 3.6 %fusion.17 = f32[8,128,1024]{2,1,0:T(8,128)} fusion(bf16[8,128,64]{1,2,0:T(8,128)(2,1)} %all-reduce.2, bf16[8,64,1024]{2,1,0:T(8,128)(2,1)S(1)} %reshape.72), kind=kOutput, calls=%fused_computation.34 | convolution fusion | flops 134217728 | bytes 5373952 | tf_op jit(solution)/shard_map/bnr,brd->bnd/dot_general | solution.py:85
  232.1 4.1 %copy.34 = bf16[16,32,2048]{2,1,0:T(8,128)(2,1)} copy(bf16[16,32,2048]{2,0,1:T(8,128)(2,1)} %bitcast.20) | data formatting | bytes 4194304 | tf_op jit(solution)/shard_map/transpose | solution.py:22
  236.2 4.1 %reshape.83 = bf16[16,64,1024]{2,1,0:T(8,128)(2,1)} reshape(bf16[16,32,2048]{2,1,0:T(8,128)(2,1)} %copy.34) | data formatting | bytes 4194304 | tf_op jit(solution)/shard_map/reshape | solution.py:22
  241.4 7.5 %all-to-all-start.7 = ((bf16[32,16,256]{2,1,0:T(8,128)(2,1)}), bf16[32,16,256]{2,1,0:T(8,128)(2,1)S(1)}, u32[]{:S(2)}, u32[]{:S(2)}) async-start(bf16[32,16,256]{2,1,0:T(8,128)(2,1)} %bitcast.24), calls=%async_computation.8 | async-start | bytes 524288 | tf_op jit(solution)/shard_map/all_to_all | solution.py:11
  248.9 7.2 %fusion = bf16[1024,1024]{1,0:T(8,128)(2,1)} fusion(f32[8,128,1024]{2,1,0:T(8,128)} %fusion.17, bf16[1024,1024]{1,0:T(8,128)(2,1)} %all-gather.5.cloned.1.call-done, bf16[1024,1024]{1,0:T(8,128)(2,1)} %param.8), kind=kOutput, calls=%fused_computation.2 | convolution fusion | flops 2149580800 | bytes 10485760 | tf_op jit(solution)/shard_map/dot_general | solution.py:79
  (47 shorter events, 21.7 us)
Async XLA Ops:
  7.2 79.4 %copy-start = (bf16[1024,1024]{1,0:T(8,128)(2,1)S(1)}, bf16[1024,1024]{1,0:T(8,128)(2,1)}, u32[]{:S(2)}) copy-start(bf16[1024,1024]{1,0:T(8,128)(2,1)} %param.7) | copy-start | bytes 6291460
  15.4 8.8 %copy-start.4 = (s32[8]{0:T(128)S(1)}, s32[8]{0:T(128)}, u32[]{:S(2)}) copy-start(s32[8]{0:T(128)} %param.11) | copy-start | bytes 100
  15.4 8.9 %copy-start.1 = (s32[512]{0:T(512)S(1)}, s32[512]{0:T(512)}, u32[]{:S(2)}) copy-start(s32[512]{0:T(512)} %param.12) | copy-start | bytes 6148
  15.4 9.5 %copy-start.5 = (u32[256]{0:T(256)S(1)}, u32[256]{0:T(256)}, u32[]{:S(2)}) copy-start(u32[256]{0:T(256)} %constant.14) | copy-start | bytes 3076
  15.5 42.7 %all-to-all-start = ((bf16[32,16,2048]{2,1,0:T(8,128)(2,1)}), bf16[32,16,2048]{2,1,0:T(8,128)(2,1)}, u32[]{:S(2)}, u32[]{:S(2)}) async-start(bf16[32,16,2048]{2,1,0:T(8,128)(2,1)} %copy.29), calls=%async_computation.1 | async-start | bytes 4194304 | tf_op jit(solution)/shard_map/all_to_all | solution.py:11
  24.2 171.7 %all-gather.7.cloned.1.call-start = ((), (), s32[]{:S(2)}) async-start(), calls=%async_computation.11 | async-start | bytes 2359296 | tf_op jit(solution)/shard_map/all_gather | solution.py:74
  88.1 160.8 %all-gather.5.cloned.1.call-start = ((), (), s32[]{:S(2)}) async-start(), calls=%async_computation.10 | async-start | bytes 2359296 | tf_op jit(solution)/shard_map/all_gather | solution.py:80
  88.9 169.9 %reduce-scatter.2.cloned.1.call-start = ((), (), s32[]{:S(2)}) async-start(), calls=%async_computation.9 | async-start | bytes 4718592 | tf_op jit(solution)/shard_map/reduce_scatter | solution.py:72
  94.8 28.7 %copy-start.2 = (bf16[1024,128]{1,0:T(8,128)(2,1)S(1)}, bf16[1024,128]{1,0:T(8,128)(2,1)}, u32[]{:S(2)}) copy-start(bf16[1024,128]{1,0:T(8,128)(2,1)} %param.13) | copy-start | bytes 786436
  191.1 32.9 %all-to-all-start.5 = ((bf16[32,16,2048]{2,1,0:T(8,128)(2,1)}), bf16[32,16,2048]{2,1,0:T(8,128)(2,1)}, u32[]{:S(2)}, u32[]{:S(2)}) async-start(bf16[32,16,2048]{2,1,0:T(8,128)(2,1)} %bitcast.64), calls=%async_computation.6 | async-start | bytes 4194304 | tf_op jit(solution)/shard_map/all_to_all | solution.py:11
  224.1 16.2 %all-to-all-start.6 = ((bf16[32,8,256]{2,1,0:T(8,128)(2,1)}), bf16[32,8,256]{2,1,0:T(8,128)(2,1)S(1)}, u32[]{:S(2)}, u32[]{:S(2)}) async-start(bf16[32,8,256]{2,1,0:T(8,128)(2,1)} %bitcast.61), calls=%async_computation.7 | async-start | bytes 262144 | tf_op jit(solution)/shard_map/all_to_all | solution.py:11
  241.4 16.5 %all-to-all-start.7 = ((bf16[32,16,256]{2,1,0:T(8,128)(2,1)}), bf16[32,16,256]{2,1,0:T(8,128)(2,1)S(1)}, u32[]{:S(2)}, u32[]{:S(2)}) async-start(bf16[32,16,256]{2,1,0:T(8,128)(2,1)} %bitcast.24), calls=%async_computation.8 | async-start | bytes 524288 | tf_op jit(solution)/shard_map/all_to_all | solution.py:11
  248.9 7.2 %copy-start.3 = (bf16[8,128,64]{1,2,0:T(8,128)(2,1)S(1)}, bf16[8,128,64]{1,2,0:T(8,128)(2,1)}, u32[]{:S(2)}) copy-start(bf16[8,128,64]{1,2,0:T(8,128)(2,1)} %reduce_sum.9) | copy-start | bytes 393220
Sparse Core Ops, SparseCore 0:
  88.2 36.5 all-gather.6
  126.5 48.5 all-gather.4
  177.6 58.0 reduce-scatter.1
